TPU v7x, 128 devices: a whole 4x4x4 slice. The times are simulated.
128 devices in a mesh: tm: 8 (over y, core), height: 16 (over x, z).
Axes of the slice: x: 4, y: 4, z: 4, core: 2. Of those that a mesh axis runs over, the one named last changes fastest.
Arguments:
- stream: bfloat16 [8, 64, 160, 2240], P('tm', 'height'), may hold values from -6 to 6
- query_tokens: bfloat16 [8, 64, 160, 1120], P('tm', 'height'), may hold values from -6 to 6
- key_tokens: bfloat16 [8, 64, 160, 1120], P('tm', 'height'), may hold values from -6 to 6
- value_tokens: bfloat16 [8, 64, 160, 1120], P('tm', 'height'), may hold values from -12 to 12
- out_weight: bfloat16 [1120, 2240], replicated, may hold values from -0.1875 to 0.1875
- in_weight: bfloat16 [2240, 2, 2800], P(None, None, 'height'), may hold values from -0.125 to 0.125
- conv_weight: float32 [3, 3, 2, 2800], replicated, may hold values from -1.2 to 1.2
Outputs:
- attended: bfloat16 [8, 64, 160, 1120], P('tm', 'height')
- gated: bfloat16 [8, 64, 160, 2800], P('tm', 'height')
All inputs are finite; a program needn't handle non-finite values.
Results may differ from a plain program's by a relative error of at most 0.0074.
Values may be sent and summed in bfloat16 or wider, within the bound.
A program may use at most 128 MiB of HBM per device.

v0:
```python
import jax
import jax.numpy as jnp
from jax import lax
from jax.sharding import PartitionSpec as P

HD = 112


def cut_along(x, dim, devices):
    lengths = x.shape
    parts = x.reshape(*lengths[:dim], devices, lengths[dim] // devices, *lengths[dim + 1 :])
    return jnp.moveaxis(parts, dim, 0)


def sent_and_summed(x, axis, dim):
    parts = cut_along(x, dim, lax.axis_size(axis))
    arrived = lax.all_to_all(parts, axis, split_axis=0, concat_axis=0, tiled=True)
    return arrived.sum(axis=0)


def sent_together(arrays, axis, dim, along):
    widths = [a.shape[along] for a in arrays]
    both = jnp.concatenate(arrays, axis=along)
    out = sent_and_summed(both, axis, dim)
    return tuple(jnp.split(out, [sum(widths[:k]) for k in range(1, len(widths))], axis=along))


def collected_together(x, axis):
    leaves = jax.tree.leaves(x)
    turns = sorted(range(len(leaves)), key=lambda k: -leaves[k].size)
    width = (1, *leaves[turns[0]].shape)[-1]
    lines = [
        jnp.pad(leaves[k].reshape(-1), (0, -leaves[k].size % width)).reshape(-1, width)
        for k in turns
    ]
    both, at, found = (lax.all_gather(jnp.concatenate(lines), axis), 0, {})
    for k, line in zip(turns, lines):
        slab = both[:, at : at + len(line)].reshape(len(both), -1)
        found[k] = slab[:, : leaves[k].size].reshape(-1, *leaves[k].shape)
        at += len(line)
    numbers = iter(range(len(leaves)))
    return jax.tree.map(lambda _: found[next(numbers)], x)


def prefix(value, axis, join, neutral):
    count, mine = (lax.axis_size(axis), lax.axis_index(axis))
    pieces = collected_together(value, axis)
    total = jax.tree.map(
        lambda part, zero: jnp.full_like(part, 0) + jnp.asarray(zero, part.dtype), value, neutral
    )

    def turn(position, total):
        longer = join(total, jax.tree.map(lambda part: part[position], pieces))
        return jax.tree.map(lambda new, old: jnp.where(position < mine, new, old), longer, total)

    return lax.fori_loop(0, count - 1, turn, total)


def sent_to_all(x, axis):
    copies = jnp.broadcast_to(x, (lax.axis_size(axis), *x.shape))
    return lax.all_to_all(copies, axis, split_axis=0, concat_axis=0, tiled=True)


def laid_out(parts, dim):
    lengths = list(parts.shape[1:])
    lengths[dim] *= parts.shape[0]
    return jnp.moveaxis(parts, 0, dim).reshape(lengths)


def gathered_copies(x, axis, dim):
    parts = sent_to_all(x, axis)
    return laid_out(parts, dim)


def with_halo(x, sides, width):
    for axis, dim in sides:
        devices, length = (lax.axis_size(axis), x.shape[dim])
        up = [(i, (i + 1) % devices) for i in range(devices - 1)]
        down = [(j, i) for i, j in up]
        last = lax.slice_in_dim(x, length - width, length, axis=dim)
        leading = lax.slice_in_dim(x, 0, width, axis=dim)
        before = lax.ppermute(last, axis, up)
        after = lax.ppermute(leading, axis, down)
        x = jnp.concatenate([before, x, after], axis=dim)
    return x


def feature(array):
    wide = array.astype(jnp.float32)
    return jnp.where(wide > 0, wide + 1.0, jnp.exp(jnp.minimum(wide, 0.0)))


def depthwise(padded, kernel):
    rows = padded.shape[1] - 2
    columns = padded.shape[2] - 2
    total = jnp.zeros(padded.shape[:1] + (rows, columns) + padded.shape[3:], jnp.float32)
    for row_off in range(3):
        for col_off in range(3):
            total = (
                total
                + padded[:, row_off : row_off + rows, col_off : col_off + columns].astype(
                    jnp.float32
                )
                * kernel[row_off, col_off]
            )
    return (total[..., 0, :] * jax.nn.silu(total[..., 1, :])).astype(jnp.bfloat16)


def add_pair(earlier, later):
    return (earlier[0] + later[0], earlier[1] + later[1])


def local(stream, query_tokens, key_tokens, value_tokens, out_weight, in_weight, conv_weight):
    frames_dev, rows_dev, columns, head_cols = query_tokens.shape
    heads = head_cols // HD
    count_tok = rows_dev * columns
    highest = lax.Precision.HIGHEST
    query_map = feature(query_tokens).reshape(frames_dev, count_tok, heads, HD)
    key_map = feature(key_tokens).reshape(frames_dev, count_tok, heads, HD)
    value_map = value_tokens.astype(jnp.float32).reshape(frames_dev, count_tok, heads, HD)
    states = jnp.einsum("fnha,fnhb->fahb", key_map, value_map, precision=highest).reshape(
        frames_dev, HD, head_cols
    )
    norms = jnp.sum(key_map, axis=1).reshape(frames_dev, 1, head_cols)
    states, norms = sent_together((states, norms), "height", 2, 1)
    states = jnp.cumsum(states, axis=0)
    norms = jnp.cumsum(norms, axis=0)
    before = prefix(
        (states[-1], norms[-1]),
        "tm",
        add_pair,
        (jnp.zeros_like(states[-1]), jnp.zeros_like(norms[-1])),
    )
    states = states + before[0]
    norms = norms + before[1]
    states, norms = (gathered_copies(states, "height", 2), gathered_copies(norms, "height", 2))
    numerator = jnp.einsum(
        "fnha,fahb->fnhb", query_map, states.reshape(frames_dev, HD, heads, HD), precision=highest
    )
    denominator = jnp.einsum(
        "fnha,fha->fnh", query_map, norms.reshape(frames_dev, heads, HD), precision=highest
    )
    attended = (
        (numerator / denominator[..., None])
        .reshape(frames_dev, rows_dev, columns, head_cols)
        .astype(jnp.bfloat16)
    )
    project = jnp.dot(
        attended.reshape(-1, head_cols), out_weight, preferred_element_type=jnp.float32
    )
    mixed = (stream.astype(jnp.float32) + project.reshape(stream.shape)).astype(jnp.bfloat16)
    expanded = jnp.einsum(
        "frwd,djc->frwjc",
        mixed,
        lax.all_gather(in_weight, "height", axis=2, tiled=True),
        preferred_element_type=jnp.float32,
    ).astype(jnp.bfloat16)
    padded = with_halo(expanded, (("height", 1),), 1)
    padded = jnp.pad(padded, ((0, 0), (0, 0), (1, 1), (0, 0), (0, 0)))
    gated = depthwise(padded, conv_weight)
    return (attended, gated)


def solution(mesh):
    placed = (
        P("tm", "height", None, None),
        P("tm", "height", None, None),
        P("tm", "height", None, None),
        P("tm", "height", None, None),
        P(),
        P(None, None, "height"),
        P(),
    )
    return jax.shard_map(
        local,
        mesh=mesh,
        in_specs=placed,
        out_specs=(P("tm", "height", None, None), P("tm", "height", None, None)),
        check_vma=False,
    )
```

profile of v0, /device:TPU:0, one launch (start us, length us, event | category | flops | bytes accessed | tf_op | source)
XLA Modules:
  0.0 301.4 jit_solution(4351893791225012609)
XLA Ops:
  7.9 2.2 fusion.25
  10.1 4.4 %reshape.183 = f32[640,10,112]{2,1,0:T(8,128)} reshape(f32[1,4,160,1120]{3,2,1,0:T(8,128)S(1)} %get-tuple-element.171) | data formatting | bytes 5734400 | tf_op jit(solution)/shard_map/reshape.1
  14.4 4.5 %reshape.184 = bf16[640,10,112]{2,1,0:T(8,128)(2,1)S(1)} reshape(bf16[1,4,160,1120]{3,2,1,0:T(8,128)(2,1)} %param.12) | data formatting | bytes 2867200 | tf_op jit(solution)/shard_map/reshape
  18.9 6.3 %fusion.32 = f32[1,112,10,112]{3,1,2,0:T(8,128)S(1)} fusion(bf16[640,10,112]{2,1,0:T(8,128)(2,1)S(1)} %reshape.184, f32[640,10,112]{2,1,0:T(8,128)} %reshape.183), kind=kOutput, calls=%fused_computation.47 | convolution fusion | flops 963379200 | bytes 4802560 | tf_op jit(solution)/shard_map/fnha,fnhb->fahb/dot_general | solution.py:121
  26.1 1.4 copy.56
  27.5 8.4 %all-to-all-start = ((f32[16,1,113,70]{2,1,3,0:T(1,128)}), f32[16,1,113,70]{2,1,3,0:T(1,128)S(1)}, u32[]{:S(2)}, u32[]{:S(2)}) async-start(f32[16,1,113,70]{2,1,3,0:T(1,128)} %copy.56), calls=%async_computation | async-start | bytes 1146880 | tf_op jit(solution)/shard_map/all_to_all | solution.py:17
  35.9 16.7 %all-to-all-done = f32[16,1,113,70]{2,1,3,0:T(1,128)S(1)} async-done(((f32[16,1,113,70]{2,1,3,0:T(1,128)}), f32[16,1,113,70]{2,1,3,0:T(1,128)S(1)}, u32[]{:S(2)}, u32[]{:S(2)}) %all-to-all-start) | async-done | bytes 506272 | tf_op jit(solution)/shard_map/all_to_all | solution.py:17
  53.2 13.5 %all-gather.1 = f32[8,113,70]{1,2,0:T(8,128)S(1)} all-gather(f32[1,113,70]{1,2,0:T(8,128)S(1)} %maximum_bitcast_fusion.1), channel_id=2, replica_groups=mesh['tm'=8,'height'=16] {'tm'}, dimensions={0}, use_global_device_ids=true | all-gather | bytes 284760 | tf_op jit(solution)/shard_map/all_gather | solution.py:36
  67.0 1.2 while.16
  69.2 5.8 %all-to-all-start.2 = ((f32[16,1,1,70]{3,2,1,0:T(1,128)}), f32[16,1,1,70]{3,2,1,0:T(1,128)S(1)}, u32[]{:S(2)}, u32[]{:S(2)}) async-start(f32[16,1,1,70]{3,2,1,0:T(1,128)} %broadcast_in_dim.24), calls=%async_computation.2 | async-start | bytes 16384 | tf_op jit(solution)/shard_map/all_to_all | solution.py:61
  75.1 7.6 %all-to-all-done.2 = f32[16,1,1,70]{3,2,1,0:T(1,128)S(1)} async-done(((f32[16,1,1,70]{3,2,1,0:T(1,128)}), f32[16,1,1,70]{3,2,1,0:T(1,128)S(1)}, u32[]{:S(2)}, u32[]{:S(2)}) %all-to-all-start.2) | async-done | bytes 4512 | tf_op jit(solution)/shard_map/all_to_all | solution.py:61
  82.6 1.1 broadcast_in_dim.22
  83.8 3.8 %all-to-all-start.1 = ((f32[16,1,112,70]{2,1,3,0:T(1,128)}), f32[16,1,112,70]{2,1,3,0:T(1,128)S(1)}, u32[]{:S(2)}, u32[]{:S(2)}) async-start(f32[16,1,112,70]{2,1,3,0:T(1,128)} %broadcast_in_dim.22), calls=%async_computation.1 | async-start | bytes 1146880 | tf_op jit(solution)/shard_map/all_to_all | solution.py:61
  87.5 2.0 fusion.27
  89.6 4.4 %reshape.185 = f32[640,10,112]{2,1,0:T(8,128)} reshape(f32[1,4,160,1120]{3,2,1,0:T(8,128)S(1)} %fusion.27) | data formatting | bytes 5734400 | tf_op jit(solution)/shard_map/reshape.7
  94.0 8.1 %copy.73 = f32[640,10,112]{0,2,1:T(8,128)S(1)} copy(f32[640,10,112]{2,1,0:T(8,128)} %reshape.185) | data formatting | bytes 5734400 | tf_op jit(solution)/shard_map/reshape.7
  103.4 1.6 fusion.40
  105.0 3.5 %fusion.29 = bf16[1,640,10,112]{1,3,2,0:T(8,128)(2,1)} fusion(f32[112,10,112]{0,2,1:T(8,128)S(1)} %bitcast.141, f32[640,10,112]{0,2,1:T(8,128)S(1)} %copy.73, f32[640,10]{0,1:T(8,128)S(1)} %bitcast.142), kind=kOutput, calls=%fused_computation.44 | convolution fusion | flops 964812800 | bytes 4828160 | tf_op jit(solution)/shard_map/fnha,fahb->fnhb/dot_general | solution.py:137
  108.5 4.9 %convert_element_type.85 = bf16[4,160,1120]{1,0,2:T(4,128)(2,1)S(1)} reshape(bf16[1,640,10,112]{1,3,2,0:T(8,128)(2,1)} %fusion.29) | data formatting | bytes 2867200 | tf_op jit(solution)/shard_map/convert_element_type | solution.py:146
  113.5 8.6 %fusion.20 = bf16[4,160,2240,1]{2,1,3,0:T(8,128)(2,1)} fusion(bf16[1120,2240]{1,0:T(8,128)(2,1)} %param.13, bf16[1,4,160,2240]{3,2,1,0:T(8,128)(2,1)} %param.9, bf16[4,160,1120]{1,0,2:T(4,128)(2,1)S(1)} %convert_element_type.85), kind=kOutput, calls=%fused_computation.36 | convolution fusion | flops 3215564800 | bytes 12185600 | tf_op jit(solution)/shard_map/dot_general | solution.py:148
  122.0 60.5 %all-gather.4.cloned.1.call-done = bf16[2240,2,2800]{0,1,2:T(2,128)(2,1)} async-done(((bf16[2240,2,175]{0,1,2:T(2,128)(2,1)}), bf16[2240,2,2800]{0,1,2:T(2,128)(2,1)}) %all-gather.4.cloned.1.call-update) | async-done | bytes 25088016 | tf_op jit(solution)/shard_map/all_gather | solution.py:155
  182.6 25.4 %fusion.15 = bf16[4,160,2,2800]{3,1,2,0:T(8,128)(2,1)} fusion(bf16[4,160,2240,1]{2,1,3,0:T(8,128)(2,1)} %fusion.20, bf16[2240,2,2800]{0,1,2:T(2,128)(2,1)} %all-gather.4.cloned.1.call-done), kind=kOutput, calls=%fused_computation.26 | convolution fusion | flops 16059904000 | bytes 35123200 | tf_op jit(solution)/shard_map/frwd,djc->frwjc/dot_general | solution.py:152
  208.0 4.1 %fusion.39 = (bf16[1,1,160,2,2800]{4,2,3,1,0:T(8,128)(2,1)}, bf16[1,1,160,2,2800]{4,2,3,1,0:T(8,128)(2,1)}) fusion(bf16[1,4,160,2,2800]{4,2,3,1,0:T(8,128)(2,1)} %bitcast.133), kind=kLoop, calls=%fused_computation.66 | loop fusion | bytes 7168000 | tf_op jit(solution)/shard_map/slice | solution.py:80
  212.2 4.3 %collective-permute-start = (bf16[1,1,160,2,2800]{4,2,3,1,0:T(8,128)(2,1)}, bf16[1,1,160,2,2800]{4,2,3,1,0:T(8,128)(2,1)}, u32[]{:S(2)}, u32[]{:S(2)}) collective-permute-start(bf16[1,1,160,2,2800]{4,2,3,1,0:T(8,128)(2,1)} %get-tuple-element.169), channel_id=1, source_target_pairs={{0,1},{1,2},{2,3},{3,4},{4,5},{5,6},{6,7},{7,8},{8,9},{9,10},{10,1... | collective-permute-start | bytes 5376008 | tf_op jit(solution)/shard_map/ppermute | solution.py:82
  216.4 1.3 collective-permute-start.1
  217.8 5.2 %convert_element_type.83 = bf16[1,4,160,1120]{2,1,3,0:T(4,128)(2,1)S(1)} reshape(bf16[1,640,10,112]{1,3,2,0:T(8,128)(2,1)} %fusion.29) | data formatting | bytes 2867200 | tf_op jit(solution)/shard_map/convert_element_type | solution.py:146
  223.0 3.3 %copy.67 = bf16[1,4,160,1120]{3,2,1,0:T(8,128)(2,1)} copy(bf16[1,4,160,1120]{2,1,3,0:T(4,128)(2,1)S(1)} %convert_element_type.83) | data formatting | bytes 2867200
  226.3 27.6 %collective-permute-done = bf16[1,1,160,2,2800]{4,2,3,1,0:T(8,128)(2,1)} collective-permute-done((bf16[1,1,160,2,2800]{4,2,3,1,0:T(8,128)(2,1)}, bf16[1,1,160,2,2800]{4,2,3,1,0:T(8,128)(2,1)}, u32[]{:S(2)}, u32[]{:S(2)}) %collective-permute-start) | collective-permute-done | bytes 1792032 | tf_op jit(solution)/shard_map/ppermute | solution.py:82
  253.9 5.3 %collective-permute-done.1 = bf16[1,1,160,2,2800]{4,2,3,1,0:T(8,128)(2,1)} collective-permute-done((bf16[1,1,160,2,2800]{4,2,3,1,0:T(8,128)(2,1)}, bf16[1,1,160,2,2800]{4,2,3,1,0:T(8,128)(2,1)}, u32[]{:S(2)}, u32[]{:S(2)}) %collective-permute-start.1) | collective-permute-done | bytes 1792032 | tf_op jit(solution)/shard_map/ppermute | solution.py:83
  259.3 9.2 %fusion.12 = bf16[1,6,162,2,2800]{4,2,3,1,0:T(8,128)(2,1)S(1)} fusion(bf16[1,1,160,2,2800]{4,2,3,1,0:T(8,128)(2,1)} %collective-permute-done.1, bf16[1,4,160,2,2800]{4,2,3,1,0:T(8,128)(2,1)} %bitcast.134, bf16[1,1,160,2,2800]{4,2,3,1,0:T(8,128)(2,1)} %collective-permute-done), kind=kLoop, calls=%fused_computation.19 | loop fusion | flops 65318400 | bytes 21638400 | tf_op jit(solution)/shard_map/concatenate | solution.py:84
  268.5 18.5 %fusion.7 = f32[1,4,160,2,2800]{4,2,3,1,0:T(8,128)} fusion(bf16[4,160,2,2800]{3,1,2,0:T(8,128)(2,1)} %fusion.15, bf16[1,6,162,2,2800]{4,2,3,1,0:T(8,128)(2,1)S(1)} %fusion.12, bf16[1,1,160,2,2800]{4,2,3,1,0:T(8,128)(2,1)} %collective-permute-done.1, bf16[1,4,160,2,2800]{4,2,3,1,0:T(8,128)(2,1)} %bitcast.135, ...), kind=kLoop, calls=%fused_computation.14 | loop fusion | flops 100352000 | bytes 75465600 | tf_op jit(solution)/shard_map/add | solution.py:100
  287.0 7.5 %fusion.14 = bf16[1,4,160,2800]{3,2,1,0:T(8,128)(2,1)} fusion(f32[1,4,160,2,2800]{4,2,3,1,0:T(8,128)} %fusion.7), kind=kLoop, calls=%fused_computation.23 | loop fusion | flops 10752000 | bytes 17920000 | tf_op jit(solution)/shard_map/convert_element_type | solution.py:106
  (55 shorter events, 5.7 us)
Async XLA Ops:
  7.2 175.4 %all-gather.4.cloned.1.call-start = ((), (), s32[]{:S(2)}) async-start(), calls=%async_computation.3 | async-start | bytes 27417600 | tf_op jit(solution)/shard_map/all_gather | solution.py:155
  27.5 25.1 %all-to-all-start = ((f32[16,1,113,70]{2,1,3,0:T(1,128)}), f32[16,1,113,70]{2,1,3,0:T(1,128)S(1)}, u32[]{:S(2)}, u32[]{:S(2)}) async-start(f32[16,1,113,70]{2,1,3,0:T(1,128)} %copy.56), calls=%async_computation | async-start | bytes 1146880 | tf_op jit(solution)/shard_map/all_to_all | solution.py:17
  69.2 13.5 %all-to-all-start.2 = ((f32[16,1,1,70]{3,2,1,0:T(1,128)}), f32[16,1,1,70]{3,2,1,0:T(1,128)S(1)}, u32[]{:S(2)}, u32[]{:S(2)}) async-start(f32[16,1,1,70]{3,2,1,0:T(1,128)} %broadcast_in_dim.24), calls=%async_computation.2 | async-start | bytes 16384 | tf_op jit(solution)/shard_map/all_to_all | solution.py:61
  83.8 21.2 %all-to-all-start.1 = ((f32[16,1,112,70]{2,1,3,0:T(1,128)}), f32[16,1,112,70]{2,1,3,0:T(1,128)S(1)}, u32[]{:S(2)}, u32[]{:S(2)}) async-start(f32[16,1,112,70]{2,1,3,0:T(1,128)} %broadcast_in_dim.22), calls=%async_computation.1 | async-start | bytes 1146880 | tf_op jit(solution)/shard_map/all_to_all | solution.py:61
  208.0 9.7 %copy-start = (f32[3,3,2,2800]{3,2,1,0:T(2,128)S(1)}, f32[3,3,2,2800]{3,2,1,0:T(2,128)}, u32[]{:S(2)}) copy-start(f32[3,3,2,2800]{3,2,1,0:T(2,128)} %param.15) | copy-start | bytes 604804
  212.2 41.7 %collective-permute-start = (bf16[1,1,160,2,2800]{4,2,3,1,0:T(8,128)(2,1)}, bf16[1,1,160,2,2800]{4,2,3,1,0:T(8,128)(2,1)}, u32[]{:S(2)}, u32[]{:S(2)}) collective-permute-start(bf16[1,1,160,2,2800]{4,2,3,1,0:T(8,128)(2,1)} %get-tuple-element.169), channel_id=1, source_target_pairs={{0,1},{1,2},{2,3},{3,4},{4,5},{5,6},{6,7},{7,8},{8,9},{9,10},{10,1... | collective-permute-start | bytes 5376008 | tf_op jit(solution)/shard_map/ppermute | solution.py:82
  216.4 42.8 %collective-permute-start.1 = (bf16[1,1,160,2,2800]{4,2,3,1,0:T(8,128)(2,1)}, bf16[1,1,160,2,2800]{4,2,3,1,0:T(8,128)(2,1)}, u32[]{:S(2)}, u32[]{:S(2)}) collective-permute-start(bf16[1,1,160,2,2800]{4,2,3,1,0:T(8,128)(2,1)} %get-tuple-element.170), channel_id=1, source_target_pairs={{1,0},{2,1},{3,2},{4,3},{5,4},{6,5},{7,6},{8,7},{9,8},{10,9},{11,1... | collective-permute-start | bytes 5376008 | tf_op jit(solution)/shard_map/ppermute | solution.py:83
Sparse Core Ops, SparseCore 0:
  10.1 172.4 all-gather.3
where the time goes:
time: 302 us; the launch traced here: 301 us
  waiting for transfers between devices  118 us (39%)
  matrix products  45.5 us (15%)
  local copies, waits for them, and re-layouts  44.6 us (15%)
  other arithmetic  41.3 us (14%)
  starting transfers between devices  23.5 us (8%)
  between operations  14.2 us (5%)
  blocking collectives  13.5 us (4%)
    all_gather x1, waiting for transfers between devices, local(): lax.all_gather(in_weight, 'height', axis=2, tiled=True)  60.5 us
    ppermute x1, waiting for transfers between devices, with_halo(): before = lax.ppermute(last, axis, up)  27.6 us
    dot_general x1, matrix products, local(): jnp.einsum('frwd,djc->frwjc', mixed, lax.all_gather(in_weight, 'height',...  25.4 us
    add x1, other arithmetic, depthwise(): total + padded[:, row_off:row_off + rows, col_off:col_off + columns].asty...  18.5 us
    another operation x4, local copies, waits for them, and re-layouts  17 us
    all_to_all x1, waiting for transfers between devices, sent_and_summed(): lax.all_to_all(parts, axis, split_axis=0, concat_axis=0, tiled=True)  16.7 us
    all_gather x1, blocking collectives, collected_together(): both, at, found = (lax.all_gather(jnp.concatenate(lines), axis), 0, {})  13.5 us
    convert_element_type x2, local copies, waits for them, and re-layouts, local(): attended = (numerator / denominator[..., None]).reshape(frames_dev, rows_...  10.1 us
  transfers between devices with their start and end apart: 6, of which 5 were waited for; matrix products, arithmetic and copies ran while one was open for 22% of the time, Pallas kernels for 0%

commit v1 on v0

--- a/solution.py
+++ b/solution.py
@@ -152,7 +152,9 @@
     expanded = jnp.einsum(
         "frwd,djc->frwjc",
         mixed,
-        lax.all_gather(in_weight, "height", axis=2, tiled=True),
+        jnp.concatenate(
+            lax.all_to_all(jnp.stack([in_weight] * lax.axis_size("height")), "height", 0, 0), axis=2
+        ),
         preferred_element_type=jnp.float32,
     ).astype(jnp.bfloat16)
     padded = with_halo(expanded, (("height", 1),), 1)

time: 302 us -> 677 us (2.24)
  waiting for transfers between devices: 118 us -> 474 us
  blocking collectives: 13.5 us -> 27.8 us
  local copies, waits for them, and re-layouts: 44.6 us -> 58.9 us
  between operations: 14.2 us -> 0.85 us
    all_to_all x0 -> x1, waiting for transfers between devices: none -> 424 us  [local(): lax.all_to_all(jnp.stack([in_weight] * lax.axis_size('height')), 'height'...]
    all_gather x1 -> x0, waiting for transfers between devices: 60.5 us -> none  [local(): lax.all_gather(in_weight, 'height', axis=2, tiled=True)]
    another operation x4 -> x5, local copies, waits for them, and re-layouts: 17 us -> 32.2 us
    all_to_all x0 -> x1, blocking collectives: none -> 14.4 us  [sent_to_all(): return lax.all_to_all(copies, axis, split_axis=0, concat_axis=0, tiled=True)]
  transfers between devices with their start and end apart: 6 -> 5, of which waited for: 5 -> 5; matrix products, arithmetic and copies ran while one was open for 22% -> 6% of each run, Pallas kernels for 0% -> 0%
where the time goes in v1:
time: 677 us
  waiting for transfers between devices  474 us (70%)
  local copies, waits for them, and re-layouts  58.9 us (9%)
  matrix products  45.2 us (7%)
  other arithmetic  41.4 us (6%)
  starting transfers between devices  28 us (4%)
  blocking collectives  27.8 us (4%)
    all_to_all x1, waiting for transfers between devices, local(): lax.all_to_all(jnp.stack([in_weight] * lax.axis_size('height')), 'height'...  424 us
    dot_general x1, matrix products, local(): jnp.einsum('frwd,djc->frwjc', mixed, jnp.concatenate(lax.all_to_all(jnp.s...  25.5 us
    ppermute x1, waiting for transfers between devices, with_halo(): before = lax.ppermute(last, axis, up)  24.9 us
    add x1, other arithmetic, depthwise(): total + padded[:, row_off:row_off + rows, col_off:col_off + columns].asty...  18.6 us
    another operation x4, local copies, waits for them, and re-layouts  16.8 us
    another operation x1, local copies, waits for them, and re-layouts, local(): jnp.stack([in_weight] * lax.axis_size('height'))  15.4 us
    all_to_all x1, blocking collectives, sent_to_all(): return lax.all_to_all(copies, axis, split_axis=0, concat_axis=0, tiled=True)  14.4 us
  transfers between devices with their start and end apart: 5, of which 5 were waited for; matrix products, arithmetic and copies ran while one was open for 6% of the time, Pallas kernels for 0%

profile of v1, /device:TPU:0, one launch (start us, length us, event | category | flops | bytes accessed | tf_op | source)
XLA Modules:
  0.0 676.6 jit_solution(9943038197410115243)
XLA Ops:
  0.6 2.2 fusion.24
  2.8 4.3 reshape.193
  7.1 4.5 reshape.194
  11.6 6.3 fusion.31
  18.8 1.4 copy.59
  20.2 8.0 %all-to-all-start = ((f32[16,1,113,70]{2,1,3,0:T(1,128)}), f32[16,1,113,70]{2,1,3,0:T(1,128)S(1)}, u32[]{:S(2)}, u32[]{:S(2)}) async-start(f32[16,1,113,70]{2,1,3,0:T(1,128)} %copy.59), calls=%async_computation | async-start | bytes 1146880 | tf_op jit(solution)/shard_map/all_to_all | solution.py:17
  28.2 12.0 %all-to-all-done = f32[16,1,113,70]{2,1,3,0:T(1,128)S(1)} async-done(((f32[16,1,113,70]{2,1,3,0:T(1,128)}), f32[16,1,113,70]{2,1,3,0:T(1,128)S(1)}, u32[]{:S(2)}, u32[]{:S(2)}) %all-to-all-start) | async-done | bytes 506272 | tf_op jit(solution)/shard_map/all_to_all | solution.py:17
  40.8 13.4 %all-gather.1 = f32[8,113,70]{1,2,0:T(8,128)S(1)} all-gather(f32[1,113,70]{1,2,0:T(8,128)S(1)} %maximum_bitcast_fusion.1), channel_id=2, replica_groups=mesh['tm'=8,'height'=16] {'tm'}, dimensions={0}, use_global_device_ids=true | all-gather | bytes 284760 | tf_op jit(solution)/shard_map/all_gather | solution.py:36
  56.7 3.5 all-to-all-start.2
  60.3 7.4 %all-to-all-done.2 = f32[16,1,1,70]{3,2,1,0:T(1,128)S(1)} async-done(((f32[16,1,1,70]{3,2,1,0:T(1,128)}), f32[16,1,1,70]{3,2,1,0:T(1,128)S(1)}, u32[]{:S(2)}, u32[]{:S(2)}) %all-to-all-start.2) | async-done | bytes 4512 | tf_op jit(solution)/shard_map/all_to_all | solution.py:61
  68.0 14.4 %all_to_all.20 = f32[16,1,112,70]{2,1,3,0:T(1,128)S(1)} all-to-all(f32[16,1,112,70]{2,1,3,0:T(1,128)S(1)} %broadcast_in_dim.22), channel_id=1, replica_groups=mesh['tm'=8,'height'=16] {'height'}, dimensions={0} | all-to-all | bytes 1003520 | tf_op jit(solution)/shard_map/all_to_all | solution.py:61
  82.4 15.4 %stack.2 = bf16[16,2240,2,175]{1,2,3,0:T(2,128)(2,1)} broadcast(bf16[2240,2,175]{0,1,2:T(2,128)(2,1)S(1)} %copy-done), dimensions={1,2,3} | broadcast | bytes 26656000 | tf_op jit(solution)/shard_map/stack | solution.py:156
  97.8 5.7 all-to-all-start.3
  103.5 2.0 fusion.26
  105.6 4.3 reshape.195
  109.9 8.1 %copy.78 = f32[640,10,112]{0,2,1:T(8,128)S(1)} copy(f32[640,10,112]{2,1,0:T(8,128)} %reshape.195) | data formatting | bytes 5734400 | tf_op jit(solution)/shard_map/reshape.7
  119.2 1.6 fusion.39
  120.8 3.5 fusion.28
  124.4 4.9 convert_element_type.85
  129.3 8.3 %fusion.19 = bf16[4,160,2240,1]{2,1,3,0:T(8,128)(2,1)} fusion(bf16[1120,2240]{1,0:T(8,128)(2,1)} %param.13, bf16[1,4,160,2240]{3,2,1,0:T(8,128)(2,1)} %param.9, bf16[4,160,1120]{1,0,2:T(4,128)(2,1)S(1)} %convert_element_type.85), kind=kOutput, calls=%fused_computation.35 | convolution fusion | flops 3215564800 | bytes 12185600 | tf_op jit(solution)/shard_map/dot_general | solution.py:148
  137.6 424.4 %all-to-all-done.3 = bf16[16,2240,2,175]{1,2,3,0:T(2,128)(2,1)} async-done(((bf16[16,2240,2,175]{1,2,3,0:T(2,128)(2,1)}), bf16[16,2240,2,175]{1,2,3,0:T(2,128)(2,1)}, u32[]{:S(2)}, u32[]{:S(2)}) %all-to-all-start.3) | async-done | bytes 25088032 | tf_op jit(solution)/shard_map/all_to_all | solution.py:156
  562.1 25.5 %fusion.14 = bf16[4,160,2,2800]{3,1,2,0:T(8,128)(2,1)} fusion(bf16[4,160,2240,1]{2,1,3,0:T(8,128)(2,1)} %fusion.19, bf16[2240,2,2800,1]{0,1,2,3:T(2,128)(2,1)} %bitcast.26), kind=kOutput, calls=%fused_computation.25 | convolution fusion | flops 16059904000 | bytes 35123200 | tf_op jit(solution)/shard_map/frwd,djc->frwjc/dot_general | solution.py:152
  587.5 4.1 fusion.38
  591.7 9.5 %collective-permute-start = (bf16[1,1,160,2,2800]{4,2,3,1,0:T(8,128)(2,1)}, bf16[1,1,160,2,2800]{4,2,3,1,0:T(8,128)(2,1)}, u32[]{:S(2)}, u32[]{:S(2)}) collective-permute-start(bf16[1,1,160,2,2800]{4,2,3,1,0:T(8,128)(2,1)} %get-tuple-element.169), channel_id=1, source_target_pairs={{0,1},{1,2},{2,3},{3,4},{4,5},{5,6},{6,7},{7,8},{8,9},{9,10},{10,1... | collective-permute-start | bytes 5376008 | tf_op jit(solution)/shard_map/ppermute | solution.py:82
  601.2 1.3 collective-permute-start.1
  602.5 5.2 convert_element_type.83
  607.7 3.3 copy.71
  611.1 24.9 %collective-permute-done = bf16[1,1,160,2,2800]{4,2,3,1,0:T(8,128)(2,1)} collective-permute-done((bf16[1,1,160,2,2800]{4,2,3,1,0:T(8,128)(2,1)}, bf16[1,1,160,2,2800]{4,2,3,1,0:T(8,128)(2,1)}, u32[]{:S(2)}, u32[]{:S(2)}) %collective-permute-start) | collective-permute-done | bytes 1792032 | tf_op jit(solution)/shard_map/ppermute | solution.py:82
  635.9 5.3 collective-permute-done.1
  641.2 9.2 %fusion.11 = bf16[1,6,162,2,2800]{4,2,3,1,0:T(8,128)(2,1)S(1)} fusion(bf16[1,1,160,2,2800]{4,2,3,1,0:T(8,128)(2,1)} %collective-permute-done.1, bf16[1,4,160,2,2800]{4,2,3,1,0:T(8,128)(2,1)} %bitcast.134, bf16[1,1,160,2,2800]{4,2,3,1,0:T(8,128)(2,1)} %collective-permute-done), kind=kLoop, calls=%fused_computation.18 | loop fusion | flops 65318400 | bytes 21638400 | tf_op jit(solution)/shard_map/concatenate | solution.py:84
  650.5 18.6 %fusion.6 = f32[1,4,160,2,2800]{4,2,3,1,0:T(8,128)} fusion(bf16[4,160,2,2800]{3,1,2,0:T(8,128)(2,1)} %fusion.14, bf16[1,6,162,2,2800]{4,2,3,1,0:T(8,128)(2,1)S(1)} %fusion.11, bf16[1,1,160,2,2800]{4,2,3,1,0:T(8,128)(2,1)} %collective-permute-done.1, bf16[1,4,160,2,2800]{4,2,3,1,0:T(8,128)(2,1)} %bitcast.135, ...), kind=kLoop, calls=%fused_computation.13 | loop fusion | flops 100352000 | bytes 75465600 | tf_op jit(solution)/shard_map/add | solution.py:100
  669.1 7.5 %fusion.13 = bf16[1,4,160,2800]{3,2,1,0:T(8,128)(2,1)} fusion(f32[1,4,160,2,2800]{4,2,3,1,0:T(8,128)} %fusion.6), kind=kLoop, calls=%fused_computation.22 | loop fusion | flops 10752000 | bytes 17920000 | tf_op jit(solution)/shard_map/convert_element_type | solution.py:106
  (56 shorter events, 6.5 us)
Async XLA Ops:
  18.2 64.2 %copy-start = (bf16[2240,2,175]{0,1,2:T(2,128)(2,1)S(1)}, bf16[2240,2,175]{0,1,2:T(2,128)(2,1)}, u32[]{:S(2)}) copy-start(bf16[2240,2,175]{0,1,2:T(2,128)(2,1)} %param.14) | copy-start | bytes 4704004
  20.2 20.0 %all-to-all-start = ((f32[16,1,113,70]{2,1,3,0:T(1,128)}), f32[16,1,113,70]{2,1,3,0:T(1,128)S(1)}, u32[]{:S(2)}, u32[]{:S(2)}) async-start(f32[16,1,113,70]{2,1,3,0:T(1,128)} %copy.59), calls=%async_computation | async-start | bytes 1146880 | tf_op jit(solution)/shard_map/all_to_all | solution.py:17
  56.7 11.0 %all-to-all-start.2 = ((f32[16,1,1,70]{3,2,1,0:T(1,128)}), f32[16,1,1,70]{3,2,1,0:T(1,128)S(1)}, u32[]{:S(2)}, u32[]{:S(2)}) async-start(f32[16,1,1,70]{3,2,1,0:T(1,128)} %broadcast_in_dim.24), calls=%async_computation.2 | async-start | bytes 16384 | tf_op jit(solution)/shard_map/all_to_all | solution.py:61
  97.8 464.3 %all-to-all-start.3 = ((bf16[16,2240,2,175]{1,2,3,0:T(2,128)(2,1)}), bf16[16,2240,2,175]{1,2,3,0:T(2,128)(2,1)}, u32[]{:S(2)}, u32[]{:S(2)}) async-start(bf16[16,2240,2,175]{1,2,3,0:T(2,128)(2,1)} %stack.2), calls=%async_computation.3 | async-start | bytes 51609600 | tf_op jit(solution)/shard_map/all_to_all | solution.py:156
  587.5 14.9 %copy-start.1 = (f32[3,3,2,2800]{3,2,1,0:T(2,128)S(1)}, f32[3,3,2,2800]{3,2,1,0:T(2,128)}, u32[]{:S(2)}) copy-start(f32[3,3,2,2800]{3,2,1,0:T(2,128)} %param.15) | copy-start | bytes 604804
  591.7 44.2 %collective-permute-start = (bf16[1,1,160,2,2800]{4,2,3,1,0:T(8,128)(2,1)}, bf16[1,1,160,2,2800]{4,2,3,1,0:T(8,128)(2,1)}, u32[]{:S(2)}, u32[]{:S(2)}) collective-permute-start(bf16[1,1,160,2,2800]{4,2,3,1,0:T(8,128)(2,1)} %get-tuple-element.169), channel_id=1, source_target_pairs={{0,1},{1,2},{2,3},{3,4},{4,5},{5,6},{6,7},{7,8},{8,9},{9,10},{10,1... | collective-permute-start | bytes 5376008 | tf_op jit(solution)/shard_map/ppermute | solution.py:82
  601.2 40.0 %collective-permute-start.1 = (bf16[1,1,160,2,2800]{4,2,3,1,0:T(8,128)(2,1)}, bf16[1,1,160,2,2800]{4,2,3,1,0:T(8,128)(2,1)}, u32[]{:S(2)}, u32[]{:S(2)}) collective-permute-start(bf16[1,1,160,2,2800]{4,2,3,1,0:T(8,128)(2,1)} %get-tuple-element.170), channel_id=1, source_target_pairs={{1,0},{2,1},{3,2},{4,3},{5,4},{6,5},{7,6},{8,7},{9,8},{10,9},{11,1... | collective-permute-start | bytes 5376008 | tf_op jit(solution)/shard_map/ppermute | solution.py:83
